TPU v7x, 512 devices: a whole 4x4x16 slice. The times are simulated.
512 devices in a mesh: col: 64 (over y, x, z_lo), row: 8 (over z_hi, core).
Axes of the slice: x: 4, y: 4, z: 16 (z_hi: 4, z_lo: 4; z = z_hi * 4 + z_lo), core: 2. Of those that a mesh axis runs over, the one named last changes fastest.
Arguments:
- slab_embed: float32 [64, 4096], P(None, 'row'), may hold values from -6 to 6
- slab_probe: float32 [32, 4096], P(None, 'row'), may hold values from -6 to 6
- point_embed: float32 [64, 131072], P(None, 'col'), may hold values from -6 to 6
- point_probe: float32 [32, 131072], P(None, 'col'), may hold values from -1.2 to 1.2
- inv_scale: float32 [64], replicated, may hold values from 0.08 to 0.3
Outputs:
- slab_grad: float32 [64, 4096], P(None, 'row')
- point_grad: float32 [64, 131072], P(None, 'col')
All inputs are finite; a program needn't handle non-finite values.
Results may differ from a plain program's by a relative error of at most 0.0001.
Values sent between devices are 32-bit elements; how exact they have to be, the bound alone decides.
A program may use at most 64 MiB of HBM per device.

v0:
```python
import jax
import jax.numpy as jnp
from jax import lax
from jax.sharding import PartitionSpec as P


def local(slab_embed, slab_probe, point_embed, point_probe, inv_scale):
    hp = lax.Precision.HIGHEST
    weight_sq = inv_scale * inv_scale
    scaled = slab_embed * weight_sq[:, None]
    self_term = jnp.sum(scaled * slab_embed, axis=0)
    points_here = point_embed.shape[1]
    width = min(1024, points_here)
    row_total = jnp.zeros((slab_embed.shape[1],), jnp.float32)
    mixed = jnp.zeros(slab_embed.shape, jnp.float32)
    pieces = []
    for block in range(points_here // width):
        points = point_embed[:, block * width : (block + 1) * width]
        probes = point_probe[:, block * width : (block + 1) * width]
        other_term = jnp.sum(weight_sq[:, None] * points * points, axis=0)
        cross = jnp.dot(scaled.T, points, precision=hp)
        kernel = jnp.exp(-0.5 * (self_term[:, None] + other_term[None, :] - 2.0 * cross))
        weights = kernel * jnp.dot(slab_probe.T, probes, precision=hp)
        row_total = row_total + jnp.sum(weights, axis=1)
        mixed = mixed + jnp.dot(points, weights.T, precision=hp)
        pieces.append(
            weight_sq[:, None]
            * (
                jnp.dot(slab_embed, weights, precision=hp)
                - points * jnp.sum(weights, axis=0)[None, :]
            )
        )
    slab_terms = -weight_sq[:, None] * (slab_embed * row_total[None, :] - mixed)
    point_terms = jnp.concatenate(pieces, axis=1)
    slab_grad = lax.psum(slab_terms, "col")
    point_grad = lax.psum(point_terms, "row")
    return (slab_grad, point_grad)


def solution(mesh):
    placed = (P(None, "row"), P(None, "row"), P(None, "col"), P(None, "col"), P())
    return jax.shard_map(
        local,
        mesh=mesh,
        in_specs=placed,
        out_specs=(P(None, "row"), P(None, "col")),
        check_vma=False,
    )
```

profile of v0, /device:TPU:1, one launch (start us, length us, event | category | flops | bytes accessed | tf_op | source)
XLA Modules:
  0.0 783.1 jit_solution(10574615676581666491)
XLA Ops:
  7.2 0.0 copy-start
  7.2 0.0 copy-start.4
  7.2 0.0 copy-start.3
  7.2 0.0 all-reduce.3.cloned.1.call-start
  7.2 0.7 multiply_negate_fusion
  8.0 1.0 fusion.18
  9.0 1.2 fusion.8
  10.2 0.0 copy-start.5
  10.2 3.0 fusion.14
  13.2 0.0 copy-done.4
  13.2 0.0 copy-done.3
  13.2 1.9 fusion.10
  15.1 0.0 copy-done
  15.1 0.0 copy-done.5
  15.1 2.4 fusion.23
  17.5 2.2 fusion.12
  19.6 2.4 fusion.24
  22.0 0.0 copy-start.1
  22.1 1.3 copy-done.1
  23.4 2.8 fusion.6
  26.2 0.0 all-reduce.3.cloned.1.call-update
  26.2 0.2 all-reduce.5.cloned.1.call-start
  26.5 0.0 copy-start.2
  26.5 1.5 fusion.3
  27.9 0.1 copy-done.2
  28.1 1.5 fusion.1
  29.5 0.8 pad_maximum_fusion
  30.3 0.0 all-reduce.5.cloned.1.call-update
  30.4 622.6 %all-reduce.3.cloned.1.call-done = f32[64,512]{1,0:T(8,128)} async-done(((f32[64,512]{1,0:T(8,128)}), f32[64,512]{1,0:T(8,128)}) %all-reduce.3.cloned.1.call-update) | async-done | bytes 131088 | tf_op jit(solution)/shard_map/psum | solution.py:35
  652.9 119.9 %all-reduce.5.cloned.1.call-done = f32[64,2048]{1,0:T(8,128)} async-done(((f32[64,2048]{1,0:T(8,128)}), f32[64,2048]{1,0:T(8,128)}) %all-reduce.5.cloned.1.call-update) | async-done | bytes 524304 | tf_op jit(solution)/shard_map/psum | solution.py:36
  772.8 1.6 copy.9
  774.4 1.9 copy.10
  (1 shorter events, 0.0 us)
Async XLA Ops:
  7.2 7.9 %copy-start = (f32[32,512]{1,0:T(8,128)S(1)}, f32[32,512]{1,0:T(8,128)}, u32[]{:S(2)}) copy-start(f32[32,512]{1,0:T(8,128)} %param.6) | copy-start | bytes 196612
  7.2 6.0 copy-start.4
  7.2 6.0 copy-start.3
  7.2 645.7 %all-reduce.3.cloned.1.call-start = ((), (), s32[]{:S(2)}) async-start(), calls=%async_computation | async-start | bytes 262144 | tf_op jit(solution)/shard_map/psum | solution.py:35
  10.2 4.9 copy-start.5
  22.0 1.4 copy-start.1
  26.2 746.6 %all-reduce.5.cloned.1.call-start = ((), (), s32[]{:S(2)}) async-start(), calls=%async_computation.1 | async-start | bytes 1048576 | tf_op jit(solution)/shard_map/psum | solution.py:36
  26.5 1.6 copy-start.2
Sparse Core Ops, SparseCore 0:
  26.4 626.5 all-reduce.2
  656.7 116.1 all-reduce.4
where the time goes:
time: 783 us
  waiting for transfers between devices  743 us (95%)
  matrix products  17.5 us (2%)
  between operations  14.1 us (2%)
    psum x1, waiting for transfers between devices, local(): slab_grad = lax.psum(slab_terms, 'col')  623 us
    psum x1, waiting for transfers between devices, local(): point_grad = lax.psum(point_terms, 'row')  120 us
  transfers between devices with their start and end apart: 2, of which 2 were waited for; matrix products, arithmetic and copies ran while one was open for 0% of the time, Pallas kernels for 0%

commit v1 on v0

--- a/solution.py
+++ b/solution.py
@@ -1,7 +1,16 @@
+import functools
 import jax
 import jax.numpy as jnp
 from jax import lax
 from jax.sharding import PartitionSpec as P
+
+
+def compute_page(in_array, shard_axis):
+    kept_arr = lax.all_gather(in_array, axis_name=shard_axis)
+    return jnp.sum(kept_arr, axis=0)
+
+
+load_matrix = functools.partial(compute_page, shard_axis="col")
 
 
 def local(slab_embed, slab_probe, point_embed, point_probe, inv_scale):
@@ -32,7 +41,7 @@
         )
     slab_terms = -weight_sq[:, None] * (slab_embed * row_total[None, :] - mixed)
     point_terms = jnp.concatenate(pieces, axis=1)
-    slab_grad = lax.psum(slab_terms, "col")
+    slab_grad = load_matrix(slab_terms)
     point_grad = lax.psum(point_terms, "row")
     return (slab_grad, point_grad)
 

time: 783 us -> 430 us (0.55)
  the two profiles are of different devices: /device:TPU:1 before, /device:TPU:128 now
where the time goes in v1:
time: 430 us
  waiting for transfers between devices  385 us (90%)
  matrix products  17.5 us (4%)
  between operations  15.6 us (4%)
  other arithmetic  8.47 us (2%)
    all_gather x1, waiting for transfers between devices, compute_page(): kept_arr = lax.all_gather(in_array, axis_name=shard_axis)  385 us
  transfers between devices with their start and end apart: 2, of which 1 were waited for; matrix products, arithmetic and copies ran while one was open for 2% of the time, Pallas kernels for 0%

profile of v1, /device:TPU:128, one launch (start us, length us, event | category | flops | bytes accessed | tf_op | source)
XLA Modules:
  0.0 430.1 jit_solution(4431955149218937922)
XLA Ops:
  8.0 0.0 copy-start
  8.0 0.0 copy-start.4
  8.0 0.0 copy-start.3
  8.0 0.0 all-gather.3.cloned.1.call-start
  8.1 0.7 multiply_negate_fusion
  8.8 1.0 fusion.18
  9.8 1.2 fusion.8
  11.0 0.0 copy-start.5
  11.0 3.0 fusion.14
  14.0 0.0 copy-done.4
  14.0 0.0 copy-done.3
  14.0 1.9 fusion.10
  15.9 0.0 copy-done
  15.9 0.0 copy-done.5
  15.9 2.4 fusion.23
  18.3 2.2 fusion.12
  20.5 2.4 fusion.24
  22.9 0.0 copy-start.1
  22.9 1.4 copy-done.1
  24.3 2.8 fusion.6
  27.1 0.0 all-gather.3.cloned.1.call-update
  27.1 0.2 all-reduce.2.cloned.1.call-start
  27.3 0.0 copy-start.2
  27.3 1.5 fusion.3
  28.8 0.1 copy-done.2
  28.9 1.5 fusion.1
  30.4 0.8 pad_maximum_fusion
  31.2 0.0 all-reduce.2.cloned.1.call-update
  31.2 384.8 %all-gather.3.cloned.1.call-done = f32[4096,512]{1,0:T(8,128)} async-done(((f32[64,512]{1,0:T(8,128)}), f32[4096,512]{1,0:T(8,128)}) %all-gather.3.cloned.1.call-update) | async-done | bytes 8388624 | tf_op jit(solution)/shard_map/all_gather | solution.py:9
  416.0 4.7 %reduce_sum.77 = f32[64,512]{1,0:T(8,128)} reduce(f32[64,64,512]{2,1,0:T(8,128)} %bitcast.27, f32[]{:T(128)} %constant.0.clone.1), dimensions={0}, to_apply=%region_5.0 | reduce | flops 2064384 | bytes 8519684 | tf_op jit(solution)/shard_map/reduce_sum | solution.py:10
  420.8 0.0 all-reduce.2.cloned.1.call-done
  420.8 1.9 copy.8
  (1 shorter events, 0.0 us)
Async XLA Ops:
  8.0 7.9 %copy-start = (f32[32,512]{1,0:T(8,128)S(1)}, f32[32,512]{1,0:T(8,128)}, u32[]{:S(2)}) copy-start(f32[32,512]{1,0:T(8,128)} %param.6) | copy-start | bytes 196612
  8.0 6.0 %copy-start.4 = (f32[64,512]{1,0:T(8,128)S(1)}, f32[64,512]{1,0:T(8,128)}, u32[]{:S(2)}) copy-start(f32[64,512]{1,0:T(8,128)} %param.5) | copy-start | bytes 393220
  8.0 6.0 %copy-start.3 = (f32[64,2048]{1,0:T(8,128)S(1)}, f32[64,2048]{1,0:T(8,128)}, u32[]{:S(2)}) copy-start(f32[64,2048]{1,0:T(8,128)} %param.7) | copy-start | bytes 1572868
  8.0 408.0 %all-gather.3.cloned.1.call-start = ((), (), s32[]{:S(2)}) async-start(), calls=%async_computation.1 | async-start | bytes 8519680 | tf_op jit(solution)/shard_map/all_gather | solution.py:9
  11.0 4.9 %copy-start.5 = (f32[32,2048]{1,0:T(8,128)S(1)}, f32[32,2048]{1,0:T(8,128)}, u32[]{:S(2)}) copy-start(f32[32,2048]{1,0:T(8,128)} %param.8) | copy-start | bytes 786436
  22.9 1.4 copy-start.1
  27.1 393.7 %all-reduce.2.cloned.1.call-start = ((), (), s32[]{:S(2)}) async-start(), calls=%async_computation | async-start | bytes 1048576 | tf_op jit(solution)/shard_map/psum | solution.py:45
  27.3 1.6 copy-start.2
Sparse Core Ops, SparseCore 0:
  27.2 388.7 all-gather.2
Sparse Core Ops, SparseCore 1:
  31.3 107.8 all-reduce.1
